TPU v7x, 32 devices: a whole 2x2x4 slice. The times are simulated.
32 devices in a mesh: row: 8 (over z, x), col: 4 (over y, core).
Axes of the slice: x: 2, y: 2, z: 4, core: 2. Of those that a mesh axis runs over, the one named last changes fastest.
Arguments:
- matrix: float32 [16384, 16384], P('row', 'col'), may hold values from -300 to 300, as said below
Outputs:
- trailing: float32 [16384, 16384], P('row', 'col')
- reflectors: float32 [16384, 8], P('row')
Inputs may be any that keep to these rules, and one draw needn't show every extreme that they name: matrix is exactly symmetric.
All inputs are finite; a program needn't handle non-finite values.
Results may differ from a plain program's by a relative error of at most 0.00021.
Values sent between devices are 32-bit elements; how exact they have to be, the bound alone decides.
A program may use at most 128 MiB of HBM per device.

v0:
```python
import jax
import jax.numpy as jnp
from jax import lax
from jax.sharding import PartitionSpec as P

N = 16384
COLS = 8


def from_root(block, axis, source):
    block = jnp.where(lax.axis_index(axis) == source, block, jnp.zeros_like(block))
    return lax.psum(block, axis)


def precise_dot(operand, factor):
    return jnp.dot(
        operand, factor, precision=lax.Precision.HIGHEST, preferred_element_type=jnp.float32
    )


def local(matrix):
    rows_local = matrix.shape[0]
    cols_local = matrix.shape[1]
    row_index = lax.axis_index("row")
    col_index = lax.axis_index("col")
    panel = from_root(matrix[:, :COLS], "col", 0)
    whole_panel = lax.all_gather(panel, "row", axis=0, tiled=True)
    all_ids = jnp.arange(whole_panel.shape[0], dtype=jnp.int32)
    reflect = jnp.zeros((N, COLS), jnp.float32)
    companion = jnp.zeros((N, COLS), jnp.float32)
    for column in range(COLS):
        reflect_rows = lax.dynamic_slice_in_dim(reflect, row_index * rows_local, rows_local, 0)
        companion_rows = lax.dynamic_slice_in_dim(companion, row_index * rows_local, rows_local, 0)
        current = (
            whole_panel[:, column]
            - precise_dot(reflect, companion[column])
            - precise_dot(companion, reflect[column])
        )
        below_whole = jnp.where(all_ids > column, current, 0.0)
        squared = jnp.sum(below_whole * below_whole)
        leading = jnp.sum(jnp.where(all_ids == column + 1, current, 0.0))
        length = jnp.sqrt(squared)
        vector = below_whole + jnp.where(all_ids == column + 1, length, 0.0)
        scaling = 1.0 / (length * (length + leading))
        vector_rows = lax.dynamic_slice_in_dim(vector, row_index * rows_local, rows_local, 0)
        vector_cols = lax.dynamic_slice_in_dim(vector, col_index * cols_local, cols_local, 0)
        weight_comp = precise_dot(companion.T, vector)
        weight_refl = precise_dot(reflect.T, vector)
        row_image = lax.psum(precise_dot(matrix, vector_cols), "col")
        pushed = scaling * (
            row_image
            - precise_dot(reflect_rows, weight_comp)
            - precise_dot(companion_rows, weight_refl)
        )
        inner_product = lax.psum(jnp.sum(pushed * vector_rows), "row")
        update_rows = pushed - 0.5 * scaling * inner_product * vector_rows
        update = lax.all_gather(update_rows, "row", axis=0, tiled=True)
        reflect = reflect.at[:, column].set(vector)
        companion = companion.at[:, column].set(update)
    reflect_rows = lax.dynamic_slice_in_dim(reflect, row_index * rows_local, rows_local, 0)
    companion_rows = lax.dynamic_slice_in_dim(companion, row_index * rows_local, rows_local, 0)
    reflect_cols = lax.dynamic_slice_in_dim(reflect, col_index * cols_local, cols_local, 0)
    companion_cols = lax.dynamic_slice_in_dim(companion, col_index * cols_local, cols_local, 0)
    trailing = (
        matrix
        - precise_dot(reflect_rows, companion_cols.T)
        - precise_dot(companion_rows, reflect_cols.T)
    )
    return (trailing, reflect_rows)


def solution(mesh):
    placed = (P("row", "col"),)
    return jax.shard_map(
        local,
        mesh=mesh,
        in_specs=placed,
        out_specs=(P("row", "col"), P("row", None)),
        check_vma=False,
    )
```

profile of v0, /device:TPU:0, one launch (start us, length us, event | category | flops | bytes accessed | tf_op | source)
XLA Modules:
  0.0 1102.3 jit_solution(3550992194655780149)
XLA Ops:
  7.2 2.3 slice_select_fusion
  10.9 0.7 compare_reduce_fusion.5
  12.3 0.7 compare_reduce_fusion.3
  15.0 35.0 %all-reduce.4.cloned.1.call-done = f32[2048,8]{1,0:T(8,128)} async-done(((f32[2048,8]{1,0:T(8,128)}), f32[2048,8]{1,0:T(8,128)}) %all-reduce.4.cloned.1.call-update) | async-done | bytes 65552 | tf_op jit(solution)/shard_map/psum | solution.py:12
  50.0 161.0 %all_gather.27 = f32[16384,8]{1,0:T(8,128)} all-gather(f32[2048,8]{1,0:T(8,128)} %all-reduce.4.cloned.1.call-done), channel_id=1, replica_groups=mesh['row'=8,'col'=4] {'row'}, dimensions={0}, use_global_device_ids=true | all-gather | bytes 589824 | tf_op jit(solution)/shard_map/all_gather | solution.py:27
  211.0 44.8 %slice_reduce_fusion = (f32[16384]{0:T(1024)S(1)}, f32[16384]{0:T(1024)S(1)}, f32[16384]{0:T(1024)S(1)}, f32[16384]{0:T(1024)S(1)}, f32[16384]{0:T(1024)S(1)}, /...) fusion(f32[16384,8]{1,0:T(8,128)} %all_gather.27), kind=kLoop, calls=%fused_computation.1 | loop fusion | bytes 1048576 | tf_op jit(solution)/shard_map/slice | solution.py:35
  259.0 1.9 fusion.5
  261.2 30.9 %fusion.109 = f32[1,2048]{1,0:T(1,128)S(1)} fusion(f32[4096,1]{0,1:T(1,128)S(1)} %bitcast.330, f32[2048,4096]{1,0:T(8,128)} %param.33), kind=kOutput, calls=%fused_computation.248 | convolution fusion | flops 100663296 | bytes 33579008 | tf_op jit(solution)/shard_map/dot_general | solution.py:16
  292.1 5.8 psum.120
  299.2 21.0 %psum.121 = f32[]{:T(128)} all-reduce(f32[]{:T(128)} %multiply_reduce_fusion.15), channel_id=1, replica_groups=mesh['row'=8,'col'=4] {'row'}, use_global_device_ids=true, to_apply=%region_7.8 | all-reduce | flops 1 | bytes 8 | tf_op jit(solution)/shard_map/psum | solution.py:55
  320.9 30.5 %all_gather.28 = f32[16384]{0:T(1024)S(1)} all-gather(f32[2048]{0:T(1024)S(1)} %multiply_subtract_fusion.7), channel_id=1, replica_groups=mesh['row'=8,'col'=4] {'row'}, dimensions={0}, use_global_device_ids=true | all-gather | bytes 73728 | tf_op jit(solution)/shard_map/all_gather | solution.py:57
  355.4 1.2 convolution_bitcast_fusion.12
  356.6 1.2 convolution_bitcast_fusion.13
  359.1 30.9 %fusion.110 = f32[1,2048]{1,0:T(1,128)S(1)} fusion(f32[4096,1]{0,1:T(1,128)S(1)} %bitcast.323, f32[2048,4096]{1,0:T(8,128)} %param.33), kind=kOutput, calls=%fused_computation.249 | convolution fusion | flops 100663296 | bytes 33579008 | tf_op jit(solution)/shard_map/dot_general | solution.py:16
  390.0 5.8 psum.122
  396.4 17.7 %psum.123 = f32[]{:T(128)} all-reduce(f32[]{:T(128)} %get-tuple-element.236), channel_id=1, replica_groups=mesh['row'=8,'col'=4] {'row'}, use_global_device_ids=true, to_apply=%region_13.14 | all-reduce | flops 1 | bytes 8 | tf_op jit(solution)/shard_map/psum | solution.py:55
  414.8 30.5 %all_gather.29 = f32[16384]{0:T(1024)S(1)} all-gather(f32[2048]{0:T(1024)S(1)} %multiply_subtract_fusion.6), channel_id=1, replica_groups=mesh['row'=8,'col'=4] {'row'}, dimensions={0}, use_global_device_ids=true | all-gather | bytes 73728 | tf_op jit(solution)/shard_map/all_gather | solution.py:57
  446.1 1.0 scatter.59
  450.3 1.2 convolution_bitcast_fusion.10
  451.6 1.2 convolution_bitcast_fusion.11
  453.9 30.7 %fusion.111 = f32[1,2048]{1,0:T(1,128)S(1)} fusion(f32[4096,1]{0,1:T(1,128)S(1)} %bitcast.325, f32[2048,4096]{1,0:T(8,128)} %param.33), kind=kOutput, calls=%fused_computation.250 | convolution fusion | flops 100663296 | bytes 33579008 | tf_op jit(solution)/shard_map/dot_general | solution.py:16
  484.6 5.8 psum.124
  491.0 19.7 %psum.125 = f32[]{:T(128)} all-reduce(f32[]{:T(128)} %get-tuple-element.233), channel_id=1, replica_groups=mesh['row'=8,'col'=4] {'row'}, use_global_device_ids=true, to_apply=%region_19.20 | all-reduce | flops 1 | bytes 8 | tf_op jit(solution)/shard_map/psum | solution.py:55
  511.4 30.5 %all_gather.30 = f32[16384]{0:T(1024)S(1)} all-gather(f32[2048]{0:T(1024)S(1)} %multiply_subtract_fusion.5), channel_id=1, replica_groups=mesh['row'=8,'col'=4] {'row'}, dimensions={0}, use_global_device_ids=true | all-gather | bytes 73728 | tf_op jit(solution)/shard_map/all_gather | solution.py:57
  542.0 0.7 broadcast_select_fusion.9
  542.7 0.7 broadcast_select_fusion.8
  547.4 1.2 convolution_bitcast_fusion.8
  548.7 1.2 convolution_bitcast_fusion.9
  551.0 30.7 %fusion.112 = f32[1,2048]{1,0:T(1,128)S(1)} fusion(f32[4096,1]{0,1:T(1,128)S(1)} %bitcast.326, f32[2048,4096]{1,0:T(8,128)} %param.33), kind=kOutput, calls=%fused_computation.251 | convolution fusion | flops 100663296 | bytes 33579008 | tf_op jit(solution)/shard_map/dot_general | solution.py:16
  581.7 5.8 psum.126
  588.1 17.8 %psum.127 = f32[]{:T(128)} all-reduce(f32[]{:T(128)} %get-tuple-element.230), channel_id=1, replica_groups=mesh['row'=8,'col'=4] {'row'}, use_global_device_ids=true, to_apply=%region_25.26 | all-reduce | flops 1 | bytes 8 | tf_op jit(solution)/shard_map/psum | solution.py:55
  606.5 30.5 %all_gather.31 = f32[16384]{0:T(1024)S(1)} all-gather(f32[2048]{0:T(1024)S(1)} %multiply_subtract_fusion.4), channel_id=1, replica_groups=mesh['row'=8,'col'=4] {'row'}, dimensions={0}, use_global_device_ids=true | all-gather | bytes 73728 | tf_op jit(solution)/shard_map/all_gather | solution.py:57
  637.1 0.8 broadcast_select_fusion.7
  637.8 0.8 broadcast_select_fusion.6
  642.7 1.2 convolution_bitcast_fusion.6
  643.9 1.2 convolution_bitcast_fusion.7
  646.3 30.7 %fusion.113 = f32[1,2048]{1,0:T(1,128)S(1)} fusion(f32[4096,1]{0,1:T(1,128)S(1)} %bitcast.327, f32[2048,4096]{1,0:T(8,128)} %param.33), kind=kOutput, calls=%fused_computation.252 | convolution fusion | flops 100663296 | bytes 33579008 | tf_op jit(solution)/shard_map/dot_general | solution.py:16
  676.9 5.8 psum.128
  683.3 19.7 %psum.129 = f32[]{:T(128)} all-reduce(f32[]{:T(128)} %get-tuple-element.227), channel_id=1, replica_groups=mesh['row'=8,'col'=4] {'row'}, use_global_device_ids=true, to_apply=%region_31.32 | all-reduce | flops 1 | bytes 8 | tf_op jit(solution)/shard_map/psum | solution.py:55
  703.7 30.5 %all_gather.32 = f32[16384]{0:T(1024)S(1)} all-gather(f32[2048]{0:T(1024)S(1)} %multiply_subtract_fusion.3), channel_id=1, replica_groups=mesh['row'=8,'col'=4] {'row'}, dimensions={0}, use_global_device_ids=true | all-gather | bytes 73728 | tf_op jit(solution)/shard_map/all_gather | solution.py:57
  735.0 0.7 broadcast_select_fusion.4
  735.7 0.9 scatter.69
  739.9 1.2 convolution_bitcast_fusion.4
  741.2 1.2 convolution_bitcast_fusion.5
  743.5 30.7 %fusion.114 = f32[1,2048]{1,0:T(1,128)S(1)} fusion(f32[4096,1]{0,1:T(1,128)S(1)} %bitcast.328, f32[2048,4096]{1,0:T(8,128)} %param.33), kind=kOutput, calls=%fused_computation.253 | convolution fusion | flops 100663296 | bytes 33579008 | tf_op jit(solution)/shard_map/dot_general | solution.py:16
  774.2 5.9 psum.130
  780.7 17.7 %psum.131 = f32[]{:T(128)} all-reduce(f32[]{:T(128)} %get-tuple-element.224), channel_id=1, replica_groups=mesh['row'=8,'col'=4] {'row'}, use_global_device_ids=true, to_apply=%region_37.38 | all-reduce | flops 1 | bytes 8 | tf_op jit(solution)/shard_map/psum | solution.py:55
  799.1 30.5 %all_gather.33 = f32[16384]{0:T(1024)S(1)} all-gather(f32[2048]{0:T(1024)S(1)} %multiply_subtract_fusion.2), channel_id=1, replica_groups=mesh['row'=8,'col'=4] {'row'}, dimensions={0}, use_global_device_ids=true | all-gather | bytes 73728 | tf_op jit(solution)/shard_map/all_gather | solution.py:57
  830.4 0.7 broadcast_select_fusion.2
  835.1 1.2 convolution_bitcast_fusion.2
  836.3 1.2 convolution_bitcast_fusion.3
  838.7 30.7 %fusion.115 = f32[1,2048]{1,0:T(1,128)S(1)} fusion(f32[4096,1]{0,1:T(1,128)S(1)} %bitcast.329, f32[2048,4096]{1,0:T(8,128)} %param.33), kind=kOutput, calls=%fused_computation.254 | convolution fusion | flops 100663296 | bytes 33579008 | tf_op jit(solution)/shard_map/dot_general | solution.py:16
  869.4 5.9 psum.132
  875.9 19.7 %psum.133 = f32[]{:T(128)} all-reduce(f32[]{:T(128)} %get-tuple-element.221), channel_id=1, replica_groups=mesh['row'=8,'col'=4] {'row'}, use_global_device_ids=true, to_apply=%region_42.43 | all-reduce | flops 1 | bytes 8 | tf_op jit(solution)/shard_map/psum | solution.py:55
  896.3 30.5 %all_gather.34 = f32[16384]{0:T(1024)S(1)} all-gather(f32[2048]{0:T(1024)S(1)} %multiply_subtract_fusion.1), channel_id=1, replica_groups=mesh['row'=8,'col'=4] {'row'}, dimensions={0}, use_global_device_ids=true | all-gather | bytes 73728 | tf_op jit(solution)/shard_map/all_gather | solution.py:57
  932.2 1.2 convolution_bitcast_fusion
  933.4 1.2 convolution_bitcast_fusion.1
  935.8 30.7 %fusion.116 = f32[1,2048]{1,0:T(1,128)S(1)} fusion(f32[4096,1]{0,1:T(1,128)S(1)} %bitcast.324, f32[2048,4096]{1,0:T(8,128)} %param.33), kind=kOutput, calls=%fused_computation.255 | convolution fusion | flops 100663296 | bytes 33579008 | tf_op jit(solution)/shard_map/dot_general | solution.py:16
  966.5 5.9 psum.134
  973.5 17.8 %psum.135 = f32[]{:T(128)} all-reduce(f32[]{:T(128)} %get-tuple-element.218), channel_id=1, replica_groups=mesh['row'=8,'col'=4] {'row'}, use_global_device_ids=true, to_apply=%region_47.48 | all-reduce | flops 1 | bytes 8 | tf_op jit(solution)/shard_map/psum | solution.py:55
  991.9 30.5 %all_gather.35 = f32[16384]{0:T(1024)S(1)} all-gather(f32[2048]{0:T(1024)S(1)} %multiply_subtract_fusion), channel_id=1, replica_groups=mesh['row'=8,'col'=4] {'row'}, dimensions={0}, use_global_device_ids=true | all-gather | bytes 73728 | tf_op jit(solution)/shard_map/all_gather | solution.py:57
  1022.4 0.7 scatter.79
  1023.2 30.3 %fusion.20 = f32[2048,4096]{1,0:T(8,128)} fusion(f32[2048,8]{0,1:T(8,128)S(1)} %constant_dynamic-slice_fusion, f32[16384,8]{0,1:T(8,128)S(1)} %scatter.79, s32[]{:T(128)S(6)} %select_n.125), kind=kOutput, calls=%fused_computation.51 | convolution fusion | flops 805306368 | bytes 33751044 | tf_op jit(solution)/shard_map/dot_general | solution.py:16
  1053.5 41.4 %subtract_subtract_fusion = f32[2048,4096]{1,0:T(8,128)} fusion(f32[2048,4096]{1,0:T(8,128)} %param.33, f32[2048,4096]{1,0:T(8,128)} %fusion.20, f32[16384,8]{0,1:T(8,128)S(1)} %scatter.76, s32[]{:T(128)S(6)} %select_n.125, f32[16384,8]{0,1:T(8,128)S(1)} %scatter.79, s32[]{:T(128)S(6)} %select_n.126), kind=kOutput, calls=%fused_computation | convolution fusion | flops 822083584 | bytes 100859912 | tf_op jit(solution)/shard_map/dot_general | solution.py:16
  (114 shorter events, 40.2 us)
Async XLA Ops:
  7.2 42.8 %all-reduce.4.cloned.1.call-start = ((), (), s32[]{:S(2)}) async-start(), calls=%async_computation | async-start | bytes 2097152 | tf_op jit(solution)/shard_map/psum | solution.py:12
  1023.2 71.7 %copy-start = (f32[2048,8]{0,1:T(8,128)}, f32[2048,8]{0,1:T(8,128)S(1)}, u32[]{:S(2)}) copy-start(f32[2048,8]{0,1:T(8,128)S(1)} %constant_dynamic-slice_fusion) | copy-start | bytes 196612
Sparse Core Ops, SparseCore 0:
  10.9 39.0 all-reduce.3
where the time goes:
time: 1110 us; the launch traced here: 1100 us
  blocking collectives  603 us (54%)
  matrix products  348 us (31%)
  local copies, waits for them, and re-layouts  57.5 us (5%)
  waiting for transfers between devices  35 us (3%)
  between operations  31.6 us (3%)
  other arithmetic  27.5 us (2%)
    dot_general x53, matrix products, precise_dot(): jnp.dot(operand, factor, precision=lax.Precision.HIGHEST, preferred_eleme...  348 us
    all_gather x8, blocking collectives, local(): update = lax.all_gather(update_rows, 'row', axis=0, tiled=True)  244 us
    all_gather x1, blocking collectives, local(): whole_panel = lax.all_gather(panel, 'row', axis=0, tiled=True)  161 us
    psum x8, blocking collectives, local(): inner_product = lax.psum(jnp.sum(pushed * vector_rows), 'row')  151 us
    psum x8, blocking collectives, local(): row_image = lax.psum(precise_dot(matrix, vector_cols), 'col')  46.5 us
    slice x1, local copies, waits for them, and re-layouts, local(): whole_panel[:, column] - precise_dot(reflect, companion[column])  44.8 us
    psum x1, waiting for transfers between devices, from_root(): return lax.psum(block, axis)  35 us
  transfers between devices with their start and end apart: 1, of which 1 were waited for; matrix products, arithmetic and copies ran while one was open for 0% of the time, Pallas kernels for 0%

commit v1 on v0

--- a/solution.py
+++ b/solution.py
@@ -1,11 +1,15 @@
+import functools
+
 import jax
 import jax.numpy as jnp
 from jax import lax
+from jax.experimental import pallas as pl
+from jax.experimental.pallas import tpu as pltpu
 from jax.sharding import PartitionSpec as P
 
-N = 16384
 COLS = 8
-
+LANES = 128
+MESH = pl.DeviceIdType.MESH
 
 def from_root(block, axis, source):
     block = jnp.where(lax.axis_index(axis) == source, block, jnp.zeros_like(block))
@@ -18,7 +22,7 @@
     )
 
 
-def local(matrix):
+def local_general(matrix):
     rows_local = matrix.shape[0]
     cols_local = matrix.shape[1]
     row_index = lax.axis_index("row")
@@ -26,8 +30,8 @@
     panel = from_root(matrix[:, :COLS], "col", 0)
     whole_panel = lax.all_gather(panel, "row", axis=0, tiled=True)
     all_ids = jnp.arange(whole_panel.shape[0], dtype=jnp.int32)
-    reflect = jnp.zeros((N, COLS), jnp.float32)
-    companion = jnp.zeros((N, COLS), jnp.float32)
+    reflect = jnp.zeros((all_ids.shape[0], COLS), jnp.float32)
+    companion = jnp.zeros((all_ids.shape[0], COLS), jnp.float32)
     for column in range(COLS):
         reflect_rows = lax.dynamic_slice_in_dim(reflect, row_index * rows_local, rows_local, 0)
         companion_rows = lax.dynamic_slice_in_dim(companion, row_index * rows_local, rows_local, 0)
@@ -69,12 +73,338 @@
     return (trailing, reflect_rows)
 
 
+def total(values):
+    folded = jnp.sum(values, axis=0)
+    return jnp.sum(jnp.sum(folded, axis=0, keepdims=True), axis=1, keepdims=True)
+
+
+def pick(values, chosen):
+    kept = jnp.where(chosen, values, 0.0)
+    return jnp.sum(jnp.sum(kept, axis=0, keepdims=True), axis=1, keepdims=True)
+
+
+def panel_kernel(
+    nr, nc, a_hbm, left_ref, right_ref,
+    a, raw, mine, panel, acc, part, arrived, image, vecs, comps, nxt, corr,
+    load_sem, scatter_sem, raw_sem, psend_sem, precv_sem,
+    send1_sem, recv1_sem, send2_sem, recv2_sem,
+):
+    r = lax.axis_index("row")
+    c = lax.axis_index("col")
+    n = nr * nc
+    rows, cols = a.shape
+    quarter = rows // nc
+    width = cols // nr
+    subs = quarter // LANES
+    tiles = cols // LANES
+    here = r * nc + c
+
+    def flip(t):
+        return t + 1 - 2 * lax.rem(t, 2)
+
+    def turn(i):
+        t = lax.rem(c + 2 * (nc // 2 - 1 - i // 2), nc)
+        own = i >= nc - 2
+        second = lax.rem(i, 2) == 1
+        first_of = jnp.where(own, flip(c), t)
+        second_of = jnp.where(own, c, flip(t))
+        return jnp.where(second, second_of, first_of)
+
+    def load(i):
+        at = pl.ds(pl.multiple_of(turn(i) * quarter, quarter), quarter)
+        return pltpu.make_async_copy(a_hbm.at[at], a.at[at], load_sem.at[i])
+
+    def rowcopy(q):
+        at = pl.ds(pl.multiple_of(q * width, width), width)
+        return a_hbm.at[pl.ds(0, COLS), at]
+
+    @pl.when(r == 0)
+    def _():
+        pltpu.make_async_copy(rowcopy(0), raw, raw_sem).start()
+
+    for i in range(nc):
+        load(i).start()
+
+    barrier = pltpu.get_barrier_semaphore()
+
+    def greet(d, carry):
+        t = lax.rem(here + d, n)
+        pl.semaphore_signal(barrier, inc=1, device_id=(t // nc, lax.rem(t, nc)), device_id_type=MESH)
+        return carry
+
+    lax.fori_loop(1, n, greet, 0)
+
+    def clear(k, carry):
+        vecs[k] = jnp.zeros(vecs.shape[1:], jnp.float32)
+        comps[k] = jnp.zeros(comps.shape[1:], jnp.float32)
+        return carry
+
+    lax.fori_loop(0, COLS + 1, clear, 0)
+    pl.semaphore_wait(barrier, n - 1)
+
+    def scatter(q):
+        return pltpu.make_async_remote_copy(
+            src_ref=rowcopy(q), dst_ref=raw, send_sem=scatter_sem.at[q], recv_sem=raw_sem,
+            device_id=(q, c), device_id_type=MESH,
+        )
+
+    @pl.when(r == 0)
+    def _():
+        for q in range(1, nr):
+            scatter(q).start()
+
+    pltpu.make_async_copy(raw, raw, raw_sem).wait()
+    for k in range(COLS):
+        for m in range(subs):
+            mine[k, m : m + 1, :] = raw[k : k + 1, m * LANES : (m + 1) * LANES]
+    spot = c * nr + r
+    panel[spot] = mine[...]
+
+    def spread(d, carry):
+        t = lax.rem(here + d, n)
+        pltpu.make_async_remote_copy(
+            src_ref=mine, dst_ref=panel.at[spot], send_sem=psend_sem, recv_sem=precv_sem,
+            device_id=(t // nc, lax.rem(t, nc)), device_id_type=MESH,
+        ).start()
+        return carry
+
+    lax.fori_loop(1, n, spread, 0)
+    most = panel.at[pl.ds(0, n - 1)]
+    pltpu.make_async_copy(most, most, precv_sem).wait()
+    pltpu.make_async_copy(most, most, psend_sem).wait()
+
+    @pl.when(r == 0)
+    def _():
+        for q in range(1, nr):
+            scatter(q).wait_send()
+
+    ids = lax.broadcasted_iota(jnp.int32, (subs, LANES), 0) * LANES + lax.broadcasted_iota(
+        jnp.int32, (subs, LANES), 1
+    )
+
+    def reflect(column, current):
+        vecs[column] = current
+        head = jnp.where(ids > column, current[0], 0.0)
+        vecs[column, 0] = head
+        below = vecs[column]
+        squared = total(below * below)
+        leading = pick(head, ids == column + 1)
+        length = jnp.sqrt(squared)
+        vecs[column, 0] = head + jnp.where(ids == column + 1, length, 0.0)
+        return 1.0 / (length * (length + leading))
+
+    def step(j, scaling):
+        vrows = [
+            jnp.broadcast_to(vecs[j, c * nr + t // subs, t % subs : t % subs + 1, :], (8, LANES))
+            for t in range(tiles)
+        ]
+
+        def block(i, carry):
+            k = turn(i)
+
+            @pl.when(j == 0)
+            def _():
+                load(i).wait()
+
+            def group(g, inner):
+                at = pl.ds(pl.multiple_of(k * quarter + g * 8, 8), 8)
+                sums = [None] * 4
+                for t in range(tiles):
+                    term = a[at, t * LANES : (t + 1) * LANES] * vrows[t]
+                    sums[t % 4] = term if sums[t % 4] is None else sums[t % 4] + term
+                acc[pl.ds(pl.multiple_of(g * 8, 8), 8), :] = (sums[0] + sums[1]) + (sums[2] + sums[3])
+                return inner
+
+            lax.fori_loop(0, quarter // 8, group, 0, unroll=4)
+            for m in range(subs):
+                turned = acc[m * LANES : (m + 1) * LANES, :].T
+                part[k, m : m + 1, :] = jnp.sum(turned, axis=0, keepdims=True)
+
+            @pl.when(i < nc - 1)
+            def _():
+                first(k).start()
+
+            return carry
+
+        def first(k):
+            return pltpu.make_async_remote_copy(
+                src_ref=part.at[k], dst_ref=arrived.at[c], send_sem=send1_sem.at[k],
+                recv_sem=recv1_sem.at[c], device_id=(r, k), device_id_type=MESH,
+            )
+
+        lax.fori_loop(0, nc, block, 0)
+        value = part[c]
+
+        def collect(d, value):
+            k = lax.rem(c + d, nc)
+            pltpu.make_async_copy(arrived.at[k], arrived.at[k], recv1_sem.at[k]).wait()
+            return value + arrived[k]
+
+        value = lax.fori_loop(1, nc, collect, value, unroll=True)
+        image[j, here] = value
+
+        def second(d, carry):
+            t = lax.rem(here + d, n)
+            pltpu.make_async_remote_copy(
+                src_ref=image.at[j, here], dst_ref=image.at[j, here], send_sem=send2_sem,
+                recv_sem=recv2_sem.at[j], device_id=(t // nc, lax.rem(t, nc)), device_id_type=MESH,
+            ).start()
+            return carry
+
+        lax.fori_loop(1, n, second, 0, unroll=True)
+
+        vector = vecs[j]
+        corr[...] = jnp.zeros(corr.shape, jnp.float32)
+        follow = jnp.minimum(j + 1, COLS - 1)
+        nxt[...] = panel[:, follow]
+        target = ids == j + 1
+
+        def history(k, carry):
+            v_k = vecs[k]
+            w_k = comps[k]
+            corr[...] = corr[...] + v_k * total(w_k * vecs[j]) + w_k * total(v_k * vecs[j])
+            nxt[...] = nxt[...] - v_k * pick(w_k[0], target) - w_k * pick(v_k[0], target)
+            return carry
+
+        lax.fori_loop(0, j, history, 0)
+
+        def sent(d, carry):
+            k = lax.rem(c + d, nc)
+            pltpu.make_async_copy(part.at[k], part.at[k], send1_sem.at[k]).wait()
+            return carry
+
+        lax.fori_loop(1, nc, sent, 0)
+        rest = image.at[j, pl.ds(0, n - 1)]
+        pltpu.make_async_copy(rest, rest, send2_sem).wait()
+        pltpu.make_async_copy(rest, rest, recv2_sem.at[j]).wait()
+
+        pushed = scaling * (image[j] - corr[...])
+        inner_product = total(pushed * vector)
+        update = pushed - (0.5 * scaling * inner_product) * vector
+        comps[j] = update
+        current = nxt[...] - vector * pick(update[0], target) - update * pick(vector[0], target)
+        return reflect(j + 1, current)
+
+    lax.fori_loop(0, COLS, step, reflect(0, panel[:, 0]))
+
+    def place(dest, base, count):
+        def move(p, carry):
+            for m in range(subs):
+                at = pl.ds(pl.multiple_of((p * subs + m) * LANES, LANES), LANES)
+                for k in range(COLS):
+                    dest[k : k + 1, at] = vecs[k, base + p, m : m + 1, :]
+                    dest[COLS + k : COLS + k + 1, at] = comps[k, base + p, m : m + 1, :]
+            return carry
+
+        lax.fori_loop(0, count, move, 0)
+
+    place(left_ref, r * nc, nc)
+    place(right_ref, c * nr, nr)
+
+
+def panel_call(nr, nc, matrix):
+    rows, cols = matrix.shape
+    n = nr * nc
+    subs = rows // nc // LANES
+    vector = (n, subs, LANES)
+    f32 = jnp.float32
+    vmem = pl.BlockSpec(memory_space=pltpu.VMEM)
+    dma = pltpu.SemaphoreType.DMA
+    return pl.pallas_call(
+        functools.partial(panel_kernel, nr, nc),
+        out_shape=(
+            jax.ShapeDtypeStruct((2 * COLS, rows), f32),
+            jax.ShapeDtypeStruct((2 * COLS, cols), f32),
+        ),
+        in_specs=[pl.BlockSpec(memory_space=pl.ANY)],
+        out_specs=(vmem, vmem),
+        scratch_shapes=[
+            pltpu.VMEM((rows, cols), f32),
+            pltpu.VMEM((COLS, cols // nr), f32),
+            pltpu.VMEM((COLS, subs, LANES), f32),
+            pltpu.VMEM((n, COLS, subs, LANES), f32),
+            pltpu.VMEM((rows // nc, LANES), f32),
+            pltpu.VMEM((nc, subs, LANES), f32),
+            pltpu.VMEM((nc, subs, LANES), f32),
+            pltpu.VMEM((COLS,) + vector, f32),
+            pltpu.VMEM((COLS + 1,) + vector, f32),
+            pltpu.VMEM((COLS + 1,) + vector, f32),
+            pltpu.VMEM(vector, f32),
+            pltpu.VMEM(vector, f32),
+            dma((nc,)), dma((nr,)), dma, dma, dma,
+            dma((nc,)), dma((nc,)), dma, dma((COLS,)),
+        ],
+        compiler_params=pltpu.CompilerParams(
+            collective_id=0, has_side_effects=True, vmem_limit_bytes=56 * 1024 * 1024
+        ),
+    )(matrix)
+
+
+def thirds(values):
+    high = values.astype(jnp.bfloat16)
+    rest = values - high.astype(jnp.float32)
+    middle = rest.astype(jnp.bfloat16)
+    low = (rest - middle.astype(jnp.float32)).astype(jnp.bfloat16)
+    return high, middle, low
+
+
+def trailing_kernel(left_ref, right_ref, a_ref, out_ref, refl_ref, stacked):
+    @pl.when(pl.program_id(0) == 0)
+    def _():
+        swapped = jnp.concatenate([right_ref[COLS:, :], right_ref[:COLS, :]], axis=0)
+        h, m, l = thirds(swapped)
+        stacked[...] = jnp.concatenate([h, m, h, m, l, h], axis=0)
+
+    left = left_ref[...]
+    h, m, l = thirds(left)
+    other = jnp.concatenate([h, h, m, m, h, l], axis=0)
+    product = lax.dot_general(
+        other, stacked[...], (((0,), (0,)), ((), ())), preferred_element_type=jnp.float32
+    )
+    out_ref[...] = a_ref[...] - product
+    refl_ref[...] = left[:COLS, :].T
+
+
+def trailing_call(left, right, matrix):
+    rows, cols = matrix.shape
+    tile = 128
+    return pl.pallas_call(
+        trailing_kernel,
+        grid=(rows // tile,),
+        out_shape=(
+            jax.ShapeDtypeStruct((rows, cols), jnp.float32),
+            jax.ShapeDtypeStruct((rows, COLS), jnp.float32),
+        ),
+        in_specs=[
+            pl.BlockSpec((2 * COLS, tile), lambda i: (0, i)),
+            pl.BlockSpec((2 * COLS, cols), lambda i: (0, 0)),
+            pl.BlockSpec((tile, cols), lambda i: (i, 0)),
+        ],
+        out_specs=(
+            pl.BlockSpec((tile, cols), lambda i: (i, 0)),
+            pl.BlockSpec((tile, COLS), lambda i: (i, 0)),
+        ),
+        scratch_shapes=[pltpu.VMEM((12 * COLS, cols), jnp.bfloat16)],
+        compiler_params=pltpu.CompilerParams(
+            dimension_semantics=("arbitrary",), vmem_limit_bytes=48 * 1024 * 1024
+        ),
+    )(left, right, matrix)
+
+
+def local(nr, nc, matrix):
+    rows, cols = matrix.shape
+    piece = rows // nc
+    if piece % LANES or piece > 8 * LANES or cols // nr != piece or nc % 2 or nr < 2:
+        return local_general(matrix)
+    left, right = panel_call(nr, nc, matrix)
+    return trailing_call(left, right, matrix)
+
+
 def solution(mesh):
-    placed = (P("row", "col"),)
     return jax.shard_map(
-        local,
+        functools.partial(local, mesh.shape["row"], mesh.shape["col"]),
         mesh=mesh,
-        in_specs=placed,
+        in_specs=(P("row", "col"),),
         out_specs=(P("row", "col"), P("row", None)),
         check_vma=False,
     )

time: 1110 us -> 128 us (0.12)
  blocking collectives: 603 us -> 0 us
  matrix products: 348 us -> 0 us
  Pallas kernels: 0 us -> 124 us
  local copies, waits for them, and re-layouts: 57.5 us -> 2.78 us
  waiting for transfers between devices: 35 us -> 0 us
  between operations: 31.6 us -> 0.65 us
  other arithmetic: 27.5 us -> 0 us
    all_gather x9 -> x0, blocking collectives: 405 us -> none  [the longest x8 244 us: local(): update = lax.all_gather(update_rows, 'row', axis=0, tiled=True)]
    dot_general x53 -> x0, matrix products: 348 us -> none  [precise_dot(): jnp.dot(operand, factor, precision=lax.Precision.HIGHEST, preferred_eleme...]
    psum x16 -> x0, blocking collectives: 198 us -> none  [the longest x8 151 us: local(): inner_product = lax.psum(jnp.sum(pushed * vector_rows), 'row')]
    pallas_call x0 -> x2, Pallas kernels: none -> 124 us  [the longest x1 95 us: panel_call(): pl.pallas_call(functools.partial(panel_kernel, nr, nc), out_shape=(jax.Sh...]
    slice x15 -> x0, local copies, waits for them, and re-layouts: 47.3 us -> none  [the longest x1 44.8 us: local(): whole_panel[:, column] - precise_dot(reflect, companion[column])]
    psum x1 -> x0, waiting for transfers between devices: 35 us -> none  [from_root(): return lax.psum(block, axis)]
    another operation x21 -> x0, other arithmetic: 14.5 us -> none
  transfers between devices with their start and end apart: 1 -> 0, of which waited for: 1 -> 0; matrix products, arithmetic and copies ran while one was open for 0% -> 0% of each run, Pallas kernels for 0% -> 0%
where the time goes in v1:
time: 128 us
  Pallas kernels  124 us (97%)
  local copies, waits for them, and re-layouts  2.78 us (2%)
    pallas_call x1, Pallas kernels, panel_call(): pl.pallas_call(functools.partial(panel_kernel, nr, nc), out_shape=(jax.Sh...  95 us
    pallas_call x1, Pallas kernels, trailing_call(): pl.pallas_call(trailing_kernel, grid=(rows // tile,), out_shape=(jax.Shap...  29.4 us

profile of v1, /device:TPU:0, one launch (start us, length us, event | category | flops | bytes accessed | tf_op | source)
XLA Modules:
  0.0 127.8 jit_solution(16589811432714614525)
XLA Ops:
  0.6 95.0 %shard_map.30 = (f32[16,2048]{1,0:T(8,128)}, f32[16,4096]{1,0:T(8,128)}) custom-call(f32[2048,4096]{1,0:T(8,128)} %a_ref.1), custom_call_target="tpu_custom_call" | custom-call | tf_op jit(solution)/shard_map/pallas_call | solution.py:313
  95.6 0.0 copy-start
  95.6 0.9 copy-done
  96.6 0.0 copy-start.1
  96.6 0.9 copy-done.1
  97.5 29.4 %shard_map.31 = (f32[2048,4096]{1,0:T(8,128)}, f32[2048,8]{1,0:T(8,128)S(1)}) custom-call(f32[16,2048]{1,0:T(8,128)S(1)} %copy-done.1, f32[16,4096]{1,0:T(8,128)S(1)} %copy-done, f32[2048,4096]{1,0:T(8,128)} %a_ref.1), custom_call_target="tpu_custom_call" | custom-call | tf_op jit(solution)/shard_map/pallas_call | solution.py:371
  126.9 0.9 copy.3
Async XLA Ops:
  95.6 1.0 copy-start
  96.6 0.9 copy-start.1

commit v2 on v1

--- a/solution.py
+++ b/solution.py
@@ -84,8 +84,8 @@
 
 
 def panel_kernel(
-    nr, nc, a_hbm, left_ref, right_ref,
-    a, raw, mine, panel, acc, part, arrived, image, vecs, comps, nxt, corr,
+    nr, nc, a_hbm, left_ref, right_ref, a,
+    raw, mine, panel, acc, part, arrived, image, vecs, comps, nxt, corr,
     load_sem, scatter_sem, raw_sem, psend_sem, precv_sem,
     send1_sem, recv1_sem, send2_sem, recv2_sem,
 ):
@@ -215,7 +215,7 @@
                 acc[pl.ds(pl.multiple_of(g * 8, 8), 8), :] = (sums[0] + sums[1]) + (sums[2] + sums[3])
                 return inner
 
-            lax.fori_loop(0, quarter // 8, group, 0, unroll=4)
+            lax.fori_loop(0, quarter // 8, group, 0, unroll=16)
             for m in range(subs):
                 turned = acc[m * LANES : (m + 1) * LANES, :].T
                 part[k, m : m + 1, :] = jnp.sum(turned, axis=0, keepdims=True)
@@ -251,7 +251,8 @@
             ).start()
             return carry
 
-        lax.fori_loop(1, n, second, 0, unroll=True)
+        for d in sorted(range(1, n), key=lambda d: abs(d - n // 2)):
+            second(d, 0)
 
         vector = vecs[j]
         corr[...] = jnp.zeros(corr.shape, jnp.float32)
@@ -315,11 +316,11 @@
         out_shape=(
             jax.ShapeDtypeStruct((2 * COLS, rows), f32),
             jax.ShapeDtypeStruct((2 * COLS, cols), f32),
+            pltpu.VMEM((rows, cols), f32),
         ),
         in_specs=[pl.BlockSpec(memory_space=pl.ANY)],
-        out_specs=(vmem, vmem),
+        out_specs=(vmem, vmem, vmem),
         scratch_shapes=[
-            pltpu.VMEM((rows, cols), f32),
             pltpu.VMEM((COLS, cols // nr), f32),
             pltpu.VMEM((COLS, subs, LANES), f32),
             pltpu.VMEM((n, COLS, subs, LANES), f32),
@@ -335,7 +336,7 @@
             dma((nc,)), dma((nc,)), dma, dma((COLS,)),
         ],
         compiler_params=pltpu.CompilerParams(
-            collective_id=0, has_side_effects=True, vmem_limit_bytes=56 * 1024 * 1024
+            collective_id=0, has_side_effects=True, vmem_limit_bytes=8 * 1024 * 1024
         ),
     )(matrix)
 
@@ -361,8 +362,9 @@
     product = lax.dot_general(
         other, stacked[...], (((0,), (0,)), ((), ())), preferred_element_type=jnp.float32
     )
-    out_ref[...] = a_ref[...] - product
-    refl_ref[...] = left[:COLS, :].T
+    at = pl.ds(pl.multiple_of(pl.program_id(0) * out_ref.shape[0], out_ref.shape[0]), out_ref.shape[0])
+    out_ref[...] = a_ref[at, :] - product
+    refl_ref[...] = left[:COLS, :]
 
 
 def trailing_call(left, right, matrix):
@@ -373,20 +375,20 @@
         grid=(rows // tile,),
         out_shape=(
             jax.ShapeDtypeStruct((rows, cols), jnp.float32),
-            jax.ShapeDtypeStruct((rows, COLS), jnp.float32),
+            jax.ShapeDtypeStruct((COLS, rows), jnp.float32),
         ),
         in_specs=[
             pl.BlockSpec((2 * COLS, tile), lambda i: (0, i)),
             pl.BlockSpec((2 * COLS, cols), lambda i: (0, 0)),
-            pl.BlockSpec((tile, cols), lambda i: (i, 0)),
+            pl.BlockSpec(memory_space=pltpu.VMEM),
         ],
         out_specs=(
             pl.BlockSpec((tile, cols), lambda i: (i, 0)),
-            pl.BlockSpec((tile, COLS), lambda i: (i, 0)),
+            pl.BlockSpec((COLS, tile), lambda i: (0, i)),
         ),
         scratch_shapes=[pltpu.VMEM((12 * COLS, cols), jnp.bfloat16)],
         compiler_params=pltpu.CompilerParams(
-            dimension_semantics=("arbitrary",), vmem_limit_bytes=48 * 1024 * 1024
+            dimension_semantics=("arbitrary",), vmem_limit_bytes=16 * 1024 * 1024
         ),
     )(left, right, matrix)
 
@@ -396,8 +398,9 @@
     piece = rows // nc
     if piece % LANES or piece > 8 * LANES or cols // nr != piece or nc % 2 or nr < 2:
         return local_general(matrix)
-    left, right = panel_call(nr, nc, matrix)
-    return trailing_call(left, right, matrix)
+    left, right, kept = panel_call(nr, nc, matrix)
+    trailing, reflectors = trailing_call(left, right, kept)
+    return trailing, reflectors.T
 
 
 def solution(mesh):

time: 128 us -> 111 us (0.87)
  Pallas kernels: 124 us -> 111 us
  local copies, waits for them, and re-layouts: 2.78 us -> 0 us
    pallas_call x1, Pallas kernels: 29.4 us -> 15.1 us  [trailing_call(): pl.pallas_call(trailing_kernel, grid=(rows // tile,), out_shape=(jax.Shap...]
    unnamed x4 -> x0, local copies, waits for them, and re-layouts: 1.85 us -> none
where the time goes in v2:
time: 111 us
  Pallas kernels  111 us (100%)
    pallas_call x1, Pallas kernels, panel_call(): pl.pallas_call(functools.partial(panel_kernel, nr, nc), out_shape=(jax.Sh...  95.5 us
    pallas_call x1, Pallas kernels, trailing_call(): pl.pallas_call(trailing_kernel, grid=(rows // tile,), out_shape=(jax.Shap...  15.1 us

profile of v2, /device:TPU:0, one launch (start us, length us, event | category | flops | bytes accessed | tf_op | source)
XLA Modules:
  0.0 111.2 jit_solution(7803208193798097524)
XLA Ops:
  0.6 95.5 %shard_map.30 = (f32[16,2048]{1,0:T(8,128)S(1)}, f32[16,4096]{1,0:T(8,128)S(1)}, f32[2048,4096]{1,0:T(8,128)S(1)}) custom-call(f32[2048,4096]{1,0:T(8,128)} %a_hbm.1), custom_call_target="tpu_custom_call" | custom-call | tf_op jit(solution)/shard_map/pallas_call | solution.py:314
  96.2 15.1 %shard_map.31 = (f32[2048,4096]{1,0:T(8,128)}, f32[8,2048]{1,0:T(8,128)}) custom-call(f32[16,2048]{1,0:T(8,128)S(1)} %get-tuple-element.7.left_ref, f32[16,4096]{1,0:T(8,128)S(1)} %get-tuple-element.8.right_ref, f32[2048,4096]{1,0:T(8,128)S(1)} %get-tuple-element.9.a_ref), custom_call_target="tpu_custom_call" | custom-call | tf_op jit(solution)/shard_map/pallas_call | solution.py:373
